TPU v7x, 32 devices: a whole 2x2x4 slice. The times are simulated.
32 devices in a mesh: tile: 8 (over z, y), chan: 4 (over x, core).
Axes of the slice: x: 2, y: 2, z: 4, core: 2. Of those that a mesh axis runs over, the one named last changes fastest.
Arguments:
- feat: bfloat16 [128, 64, 256], P('tile', 'chan'), may hold values from -6 to 6
- lift: float32 [64], replicated, may hold values from -3 to 3
- dilation4_weight: bfloat16 [3, 3, 64, 64], replicated, may hold values from -0.25 to 0.25
- dilation8_weight: bfloat16 [3, 3, 64, 64], replicated, may hold values from -0.25 to 0.25
- entry_fraction: bfloat16 [2048, 128], P('tile'), may hold values from 0.019897461 to 0.19921875
- entry_target_tile: int32 [2048, 1], P('tile'), may hold values from 0 to 7; in each aligned block of 256 rows (0 to 255, 256 to 511, ...) at most 64 rows name the same one
- entry_owner_tile: int32 [2048], P('tile'), may hold values from 0 to 31
- entry_local_net: int32 [2048], P('tile'), may hold values from 0 to 63
- pin_demand_weight: float32 [2048], P('tile'), may hold values from 0.2 to 2
- pin_local_net: int32 [2048], P('tile'), may hold values from 0 to 63
- pin_global_cell: int32 [2048], P('tile'), may hold values from 0 to 511
Outputs:
- cell_grad: float32 [512], P('tile')
Inputs may be any that keep to these rules, and one draw needn't show every extreme that they name: `entry_target_tile`: among the entries of one tile index, at most 64 name the same destination, and in some tile index exactly 64 do.
All inputs are finite; a program needn't handle non-finite values.
Results may differ from a plain program's by a relative error of at most 0.0003.
Values may be sent and summed in bfloat16 or wider, within the bound.
A program may use at most 64 MiB of HBM per device.

v0:
```python
import jax
import jax.numpy as jnp
from jax import lax
from jax.sharding import PartitionSpec as P

NET_DEV = 64
CELL_DEV = 64
TILE_DEV = 32


def extended(array, sides, width):
    for axis, dim in sides:
        peers, length = (lax.axis_size(axis), array.shape[dim])
        up = [(i, (i + 1) % peers) for i in range(peers - 1)]
        down = [(j, i) for i, j in up]
        last = lax.slice_in_dim(array, length - width, length, axis=dim)
        leading = lax.slice_in_dim(array, 0, width, axis=dim)
        before = lax.ppermute(last, axis, up)
        after = lax.ppermute(leading, axis, down)
        array = jnp.concatenate([before, array, after], axis=dim)
    return array


def flipped_kernel(kernel):
    return jnp.transpose(kernel[::-1, ::-1], (0, 1, 3, 2))


def dilated_convolution(own_part, weights, channel_start, dilation):
    row_count, chan_own, col_count = own_part.shape
    rimmed = extended(own_part, (("tile", 0),), dilation)
    own_weights = lax.dynamic_slice_in_dim(weights, channel_start, chan_own, 3)
    start_sum = jnp.zeros((row_count, chan_own, col_count), jnp.float32)
    running = start_sum
    widened = jnp.pad(
        lax.all_gather(rimmed, "chan", axis=1, tiled=True), ((0, 0), (0, 0), (dilation, dilation))
    )
    for row_tap in range(3):
        for col_tap in range(3):
            part_in = widened[
                row_tap * dilation : row_tap * dilation + row_count,
                :,
                col_tap * dilation : col_tap * dilation + col_count,
            ]
            running = running + jnp.einsum(
                "rcw,co->row",
                part_in,
                own_weights[row_tap, col_tap],
                preferred_element_type=jnp.float32,
            )
    return running


def local(
    feat,
    lift,
    dilation4_weight,
    dilation8_weight,
    entry_fraction,
    entry_target_tile,
    entry_owner_tile,
    entry_local_net,
    pin_demand_weight,
    pin_local_net,
    pin_global_cell,
):
    highest = lax.Precision.HIGHEST
    tile_count = lax.axis_size("tile")
    chan_count = lax.axis_size("chan")
    row_count, chan_own, col_count = feat.shape
    channel_start = lax.axis_index("chan") * chan_own
    lift_own = lax.dynamic_slice_in_dim(lift, channel_start, chan_own, 0)
    entry_count = entry_target_tile.shape[0]
    capacity = chan_count * max(1, 2 * entry_count // (chan_count * tile_count))
    part_total = 1
    part_id = 0
    slot_count = capacity // part_total
    destination = entry_target_tile[:, 0]
    dest_hot = (destination[:, None] == jnp.arange(tile_count, dtype=jnp.int32)[None, :]).astype(
        jnp.int32
    )
    rank = jnp.sum(jnp.cumsum(dest_hot, axis=0) * dest_hot, axis=1) - 1
    placed = rank % part_total == part_id
    slot_row = jnp.where(
        placed, destination * slot_count + rank // part_total, tile_count * slot_count
    )
    pin_hot = (pin_local_net[None, :] == jnp.arange(NET_DEV, dtype=jnp.int32)[:, None]).astype(
        jnp.float32
    )
    strength = jnp.dot(pin_hot, pin_demand_weight, precision=highest)
    entry_hot = (entry_local_net[:, None] == jnp.arange(NET_DEV, dtype=jnp.int32)[None, :]).astype(
        jnp.float32
    )
    entry_strength = jnp.dot(entry_hot, strength, precision=highest)
    frac = entry_fraction.astype(jnp.float32)
    payload = entry_strength[:, None] * frac
    send_rows = (
        jnp.zeros((tile_count * slot_count, 128), jnp.float32)
        .at[slot_row]
        .set(payload, mode="drop")
    )
    send_ids = (
        jnp.zeros((tile_count * slot_count,), jnp.int32)
        .at[slot_row]
        .set(entry_owner_tile, mode="drop")
    )
    arrived, arrived_ids = (
        lax.all_to_all(
            send_rows.reshape(tile_count, slot_count, 128).astype(jnp.bfloat16),
            "tile",
            split_axis=0,
            concat_axis=0,
            tiled=True,
        ).astype(jnp.float32),
        lax.all_to_all(
            send_ids.reshape(tile_count, slot_count),
            "tile",
            split_axis=0,
            concat_axis=0,
            tiled=True,
        ),
    )
    tile_hot = (
        arrived_ids.reshape(-1)[:, None] == jnp.arange(TILE_DEV, dtype=jnp.int32)[None, :]
    ).astype(jnp.float32)
    tiles = jnp.dot(tile_hot.T, arrived.reshape(-1, 128), precision=highest)
    demand = (
        tiles.reshape(row_count // 8, col_count // 16, 8, 16)
        .transpose(0, 2, 1, 3)
        .reshape(row_count, col_count)
    )
    input_features = (
        feat.astype(jnp.float32) + demand[:, None, :] * lift_own[None, :, None]
    ).astype(jnp.bfloat16)
    first_preactivation = dilated_convolution(input_features, dilation4_weight, channel_start, 4)
    hidden_features = jax.nn.silu(first_preactivation).astype(jnp.bfloat16)
    second_output = dilated_convolution(hidden_features, dilation8_weight, channel_start, 8)
    second_gradient = jax.nn.sigmoid(second_output).astype(jnp.bfloat16)
    hidden_gradient = dilated_convolution(
        second_gradient, flipped_kernel(dilation8_weight), channel_start, 8
    )
    sigmoid_pre = jax.nn.sigmoid(first_preactivation)
    preactivation_gradient = (
        hidden_gradient * sigmoid_pre * (1.0 + first_preactivation * (1.0 - sigmoid_pre))
    ).astype(jnp.bfloat16)
    inputs_gradient = dilated_convolution(
        preactivation_gradient, flipped_kernel(dilation4_weight), channel_start, 4
    )
    partial_grad = jnp.sum(inputs_gradient * lift_own[None, :, None], axis=1)
    grad_demand = lax.psum(partial_grad, "chan")
    grad_tiles = (
        grad_demand.reshape(row_count // 8, 8, col_count // 16, 16)
        .transpose(0, 2, 1, 3)
        .reshape(TILE_DEV, 128)
    )
    slot_grads = jnp.dot(tile_hot, grad_tiles, precision=highest).reshape(
        tile_count, slot_count, 128
    )
    returned = lax.all_to_all(
        slot_grads.astype(jnp.bfloat16), "tile", split_axis=0, concat_axis=0, tiled=True
    ).astype(slot_grads.dtype)
    entry_rows = jnp.take(returned.reshape(-1, 128), slot_row, axis=0, mode="fill", fill_value=0.0)
    entry_grad = jnp.sum(entry_rows * frac, axis=1)
    grad_net = jnp.dot(entry_grad, entry_hot, precision=highest)
    pin_grad = jnp.dot(grad_net, pin_hot, precision=highest)
    cell_term = jax.ops.segment_sum(pin_grad, pin_global_cell, num_segments=CELL_DEV * tile_count)
    return lax.psum_scatter(cell_term, "tile", scatter_dimension=0, tiled=True)


def solution(mesh):
    in_specs = (
        P("tile", "chan", None),
        P(),
        P(),
        P(),
        P("tile", None),
        P("tile", None),
        P("tile"),
        P("tile"),
        P("tile"),
        P("tile"),
        P("tile"),
    )
    out_specs = P("tile")
    return jax.shard_map(local, mesh=mesh, in_specs=in_specs, out_specs=out_specs, check_vma=False)
```

profile of v0, /device:TPU:0, one launch (start us, length us, event | category | flops | bytes accessed | tf_op | source)
XLA Modules:
  0.0 194.8 jit_solution(14243430125302070767)
XLA Ops:
  9.6 1.6 scatter_custom_fusion
  11.8 7.3 %all-to-all-start = ((s32[8,1,64]{2,1,0:T(1,128)}), s32[8,1,64]{2,1,0:T(1,128)S(1)}, u32[]{:S(2)}, u32[]{:S(2)}) async-start(s32[8,1,64]{2,1,0:T(1,128)} %all_to_all.12), calls=%async_computation | async-start | bytes 8192 | tf_op jit(solution)/shard_map/all_to_all | solution.py:114
  19.9 0.9 fusion.42
  20.8 1.7 scatter_custom_fusion.1
  23.2 2.4 %all-to-all-done = s32[8,1,64]{2,1,0:T(1,128)S(1)} async-done(((s32[8,1,64]{2,1,0:T(1,128)}), s32[8,1,64]{2,1,0:T(1,128)S(1)}, u32[]{:S(2)}, u32[]{:S(2)}) %all-to-all-start) | async-done | bytes 2080 | tf_op jit(solution)/shard_map/all_to_all | solution.py:114
  25.6 3.6 %all-to-all-start.1 = ((bf16[8,64,128]{2,1,0:T(8,128)(2,1)}), bf16[8,64,128]{2,1,0:T(8,128)(2,1)S(1)}, u32[]{:S(2)}, u32[]{:S(2)}) async-start(bf16[8,64,128]{2,1,0:T(8,128)(2,1)} %bitcast.24), calls=%async_computation.1 | async-start | bytes 262144 | tf_op jit(solution)/shard_map/all_to_all | solution.py:107
  30.5 5.9 %all-to-all-done.1 = bf16[8,64,128]{2,1,0:T(8,128)(2,1)S(1)} async-done(((bf16[8,64,128]{2,1,0:T(8,128)(2,1)}), bf16[8,64,128]{2,1,0:T(8,128)(2,1)S(1)}, u32[]{:S(2)}, u32[]{:S(2)}) %all-to-all-start.1) | async-done | bytes 131104 | tf_op jit(solution)/shard_map/all_to_all | solution.py:107
  37.2 1.3 collective-permute-start.1
  38.5 4.5 %collective-permute-start = (bf16[4,16,256]{2,1,0:T(8,128)(2,1)S(1)}, bf16[4,16,256]{2,1,0:T(8,128)(2,1)S(1)}, u32[]{:S(2)}, u32[]{:S(2)}) collective-permute-start(bf16[4,16,256]{2,1,0:T(8,128)(2,1)S(1)} %get-tuple-element.13), channel_id=1, source_target_pairs={{0,4},{4,8},{8,12},{12,16},{16,20},{20,24},{24,28},{1,5},{5,9},{9,... | collective-permute-start | bytes 98312 | tf_op jit(solution)/shard_map/ppermute | solution.py:18
  43.1 1.6 collective-permute-done
  44.7 8.6 %all_gather.12 = bf16[24,64,256]{2,1,0:T(8,128)(2,1)S(1)} all-gather(bf16[24,16,256]{2,1,0:T(8,128)(2,1)S(1)} %pad_maximum_fusion.2), channel_id=1, replica_groups=mesh['tile'=8,'chan'=4] {'chan'}, dimensions={1}, use_global_device_ids=true | all-gather | bytes 983040 | tf_op jit(solution)/shard_map/all_gather | solution.py:35
  56.4 1.3 collective-permute-start.3
  57.7 4.9 %collective-permute-start.2 = (bf16[8,16,256]{2,1,0:T(8,128)(2,1)S(1)}, bf16[8,16,256]{2,1,0:T(8,128)(2,1)S(1)}, u32[]{:S(2)}, u32[]{:S(2)}) collective-permute-start(bf16[8,16,256]{2,1,0:T(8,128)(2,1)S(1)} %get-tuple-element.11), channel_id=1, source_target_pairs={{0,4},{4,8},{8,12},{12,16},{16,20},{20,24},{24,28},{1,5},{5,9},{9,... | collective-permute-start | bytes 196616 | tf_op jit(solution)/shard_map/ppermute | solution.py:18
  63.2 1.6 collective-permute-done.2
  65.6 17.1 %all-gather.3.cloned.1.call-done = bf16[32,64,256]{2,1,0:T(8,128)(2,1)} async-done(((bf16[32,16,256]{2,1,0:T(8,128)(2,1)}), bf16[32,64,256]{2,1,0:T(8,128)(2,1)}) %all-gather.3.cloned.1.call-update) | async-done | bytes 1048592 | tf_op jit(solution)/shard_map/all_gather | solution.py:35
  82.7 1.5 fusion.33
  86.9 1.6 fusion.46
  88.6 1.3 collective-permute-start.5
  89.9 4.7 %collective-permute-start.4 = (bf16[8,16,256]{2,0,1:T(8,128)(2,1)S(1)}, bf16[8,16,256]{2,0,1:T(8,128)(2,1)S(1)}, u32[]{:S(2)}, u32[]{:S(2)}) collective-permute-start(bf16[8,16,256]{2,0,1:T(8,128)(2,1)S(1)} %get-tuple-element.9), channel_id=1, source_target_pairs={{0,4},{4,8},{8,12},{12,16},{16,20},{20,24},{24,28},{1,5},{5,9},{9,... | collective-permute-start | bytes 196616 | tf_op jit(solution)/shard_map/ppermute | solution.py:18
  94.7 1.6 collective-permute-done.4
  97.2 18.6 %all-gather.5.cloned.1.call-done = bf16[32,64,256]{2,0,1:T(8,128)(2,1)} async-done(((bf16[32,16,256]{2,0,1:T(8,128)(2,1)}), bf16[32,64,256]{2,0,1:T(8,128)(2,1)}) %all-gather.5.cloned.1.call-update) | async-done | bytes 1048592 | tf_op jit(solution)/shard_map/all_gather | solution.py:35
  115.7 1.8 copy.66
  120.1 1.3 collective-permute-start.7
  121.4 4.5 %collective-permute-start.6 = (bf16[4,16,256]{2,1,0:T(8,128)(2,1)S(1)}, bf16[4,16,256]{2,1,0:T(8,128)(2,1)S(1)}, u32[]{:S(2)}, u32[]{:S(2)}) collective-permute-start(bf16[4,16,256]{2,1,0:T(8,128)(2,1)S(1)} %get-tuple-element.7), channel_id=1, source_target_pairs={{0,4},{4,8},{8,12},{12,16},{16,20},{20,24},{24,28},{1,5},{5,9},{9,... | collective-permute-start | bytes 98312 | tf_op jit(solution)/shard_map/ppermute | solution.py:18
  126.0 1.5 collective-permute-done.6
  127.6 7.5 %all_gather.15 = bf16[24,64,256]{2,1,0:T(8,128)(2,1)S(1)} all-gather(bf16[24,16,256]{2,1,0:T(8,128)(2,1)S(1)} %pad_maximum_fusion.3), channel_id=1, replica_groups=mesh['tile'=8,'chan'=4] {'chan'}, dimensions={1}, use_global_device_ids=true | all-gather | bytes 983040 | tf_op jit(solution)/shard_map/all_gather | solution.py:35
  137.8 11.7 %psum.7 = f32[32,128]{1,0:T(8,128)S(1)} all-reduce(f32[32,128]{1,0:T(8,128)S(1)} %reshape.105), channel_id=1, replica_groups=mesh['tile'=8,'chan'=4] {'chan'}, use_global_device_ids=true, to_apply=%region_6.7 | all-reduce | flops 4096 | bytes 32768 | tf_op jit(solution)/shard_map/psum | solution.py:149
  149.6 1.0 convolution_convert_fusion
  150.6 7.4 %all-to-all-start.2 = ((bf16[8,64,128]{2,1,0:T(8,128)(2,1)}), bf16[8,64,128]{2,1,0:T(8,128)(2,1)S(1)}, u32[]{:S(2)}, u32[]{:S(2)}) async-start(bf16[8,64,128]{2,1,0:T(8,128)(2,1)} %convolution_convert_fusion), calls=%async_computation.2 | async-start | bytes 262144 | tf_op jit(solution)/shard_map/all_to_all | solution.py:158
  159.3 6.1 %all-to-all-done.2 = bf16[8,64,128]{2,1,0:T(8,128)(2,1)S(1)} async-done(((bf16[8,64,128]{2,1,0:T(8,128)(2,1)}), bf16[8,64,128]{2,1,0:T(8,128)(2,1)S(1)}, u32[]{:S(2)}, u32[]{:S(2)}) %all-to-all-start.2) | async-done | bytes 131104 | tf_op jit(solution)/shard_map/all_to_all | solution.py:158
  166.7 2.5 %scatter_custom_fusion.2 = f32[512]{0:T(512)S(1)} fusion(s32[256]{0:T(256)} %param.21, f32[256]{0:T(256)S(1)} %bitcast.284, f32[]{:T(128)} %constant.62.clone.1), kind=kCustom, calls=%fused_computation.201 | custom fusion | flops 256 | bytes 2560 | tf_op jit(solution)/shard_map/scatter-add | solution.py:165
  169.2 18.2 %all-reduce.4 = f32[512]{0:T(512)S(1)} all-reduce(f32[512]{0:T(512)S(1)} %scatter_custom_fusion.2), channel_id=2, replica_groups=mesh['tile'=8,'chan'=4] {'tile'}, use_global_device_ids=true, to_apply=%region_9.10.clone | all-reduce | flops 512 | bytes 4096
  (106 shorter events, 23.3 us)
Async XLA Ops:
  6.5 12.6 %copy-start = (f32[256]{0:T(256)S(1)}, f32[256]{0:T(256)}, u32[]{:S(2)}) copy-start(f32[256]{0:T(256)} %param.19) | copy-start | bytes 3076
  6.5 22.7 %copy-start.8 = (f32[64]{0:T(128)S(1)}, f32[64]{0:T(128)}, u32[]{:S(2)}) copy-start(f32[64]{0:T(128)} %param.12) | copy-start | bytes 772
  6.5 30.5 %copy-start.5 = (bf16[16,16,256]{2,1,0:T(8,128)(2,1)S(1)}, bf16[16,16,256]{2,1,0:T(8,128)(2,1)}, u32[]{:S(2)}) copy-start(bf16[16,16,256]{2,1,0:T(8,128)(2,1)} %param.11) | copy-start | bytes 393220
  11.8 13.8 %all-to-all-start = ((s32[8,1,64]{2,1,0:T(1,128)}), s32[8,1,64]{2,1,0:T(1,128)S(1)}, u32[]{:S(2)}, u32[]{:S(2)}) async-start(s32[8,1,64]{2,1,0:T(1,128)} %all_to_all.12), calls=%async_computation | async-start | bytes 8192 | tf_op jit(solution)/shard_map/all_to_all | solution.py:114
  25.6 10.9 %all-to-all-start.1 = ((bf16[8,64,128]{2,1,0:T(8,128)(2,1)}), bf16[8,64,128]{2,1,0:T(8,128)(2,1)S(1)}, u32[]{:S(2)}, u32[]{:S(2)}) async-start(bf16[8,64,128]{2,1,0:T(8,128)(2,1)} %bitcast.24), calls=%async_computation.1 | async-start | bytes 262144 | tf_op jit(solution)/shard_map/all_to_all | solution.py:107
  29.2 53.6 %all-gather.3.cloned.1.call-start = ((), (), s32[]{:S(2)}) async-start(), calls=%async_computation.3 | async-start | bytes 1310720 | tf_op jit(solution)/shard_map/all_gather | solution.py:35
  36.6 16.7 %copy-start.3 = (bf16[3,3,64,64]{3,2,1,0:T(8,128)(2,1)S(1)}, bf16[3,3,64,64]{3,2,1,0:T(8,128)(2,1)}, u32[]{:S(2)}) copy-start(bf16[3,3,64,64]{3,2,1,0:T(8,128)(2,1)} %param.13) | copy-start | bytes 221188
  37.2 5.9 %collective-permute-start.1 = (bf16[4,16,256]{2,1,0:T(8,128)(2,1)S(1)}, bf16[4,16,256]{2,1,0:T(8,128)(2,1)S(1)}, u32[]{:S(2)}, u32[]{:S(2)}) collective-permute-start(bf16[4,16,256]{2,1,0:T(8,128)(2,1)S(1)} %get-tuple-element.14), channel_id=1, source_target_pairs={{4,0},{8,4},{12,8},{16,12},{20,16},{24,20},{28,24},{5,1},{9,5},{13... | collective-permute-start | bytes 98312 | tf_op jit(solution)/shard_map/ppermute | solution.py:19
  38.5 6.1 %collective-permute-start = (bf16[4,16,256]{2,1,0:T(8,128)(2,1)S(1)}, bf16[4,16,256]{2,1,0:T(8,128)(2,1)S(1)}, u32[]{:S(2)}, u32[]{:S(2)}) collective-permute-start(bf16[4,16,256]{2,1,0:T(8,128)(2,1)S(1)} %get-tuple-element.13), channel_id=1, source_target_pairs={{0,4},{4,8},{8,12},{12,16},{16,20},{20,24},{24,28},{1,5},{5,9},{9,... | collective-permute-start | bytes 98312 | tf_op jit(solution)/shard_map/ppermute | solution.py:18
  56.0 26.7 %copy-start.2 = (bf16[3,3,64,64]{3,2,1,0:T(8,128)(2,1)S(1)}, bf16[3,3,64,64]{3,2,1,0:T(8,128)(2,1)}, u32[]{:S(2)}) copy-start(bf16[3,3,64,64]{3,2,1,0:T(8,128)(2,1)} %param.14) | copy-start | bytes 221188
  56.4 6.8 %collective-permute-start.3 = (bf16[8,16,256]{2,1,0:T(8,128)(2,1)S(1)}, bf16[8,16,256]{2,1,0:T(8,128)(2,1)S(1)}, u32[]{:S(2)}, u32[]{:S(2)}) collective-permute-start(bf16[8,16,256]{2,1,0:T(8,128)(2,1)S(1)} %get-tuple-element.12), channel_id=1, source_target_pairs={{4,0},{8,4},{12,8},{16,12},{20,16},{24,20},{28,24},{5,1},{9,5},{13... | collective-permute-start | bytes 196616 | tf_op jit(solution)/shard_map/ppermute | solution.py:19
  57.7 7.1 %collective-permute-start.2 = (bf16[8,16,256]{2,1,0:T(8,128)(2,1)S(1)}, bf16[8,16,256]{2,1,0:T(8,128)(2,1)S(1)}, u32[]{:S(2)}, u32[]{:S(2)}) collective-permute-start(bf16[8,16,256]{2,1,0:T(8,128)(2,1)S(1)} %get-tuple-element.11), channel_id=1, source_target_pairs={{0,4},{4,8},{8,12},{12,16},{16,20},{20,24},{24,28},{1,5},{5,9},{9,... | collective-permute-start | bytes 196616 | tf_op jit(solution)/shard_map/ppermute | solution.py:18
  65.6 50.2 %all-gather.5.cloned.1.call-start = ((), (), s32[]{:S(2)}) async-start(), calls=%async_computation.4 | async-start | bytes 1310720 | tf_op jit(solution)/shard_map/all_gather | solution.py:35
  82.7 1.5 copy-start.1
  88.6 6.2 %collective-permute-start.5 = (bf16[8,16,256]{2,0,1:T(8,128)(2,1)S(1)}, bf16[8,16,256]{2,0,1:T(8,128)(2,1)S(1)}, u32[]{:S(2)}, u32[]{:S(2)}) collective-permute-start(bf16[8,16,256]{2,0,1:T(8,128)(2,1)S(1)} %get-tuple-element.10), channel_id=1, source_target_pairs={{4,0},{8,4},{12,8},{16,12},{20,16},{24,20},{28,24},{5,1},{9,5},{13... | collective-permute-start | bytes 196616 | tf_op jit(solution)/shard_map/ppermute | solution.py:19
  89.9 6.4 %collective-permute-start.4 = (bf16[8,16,256]{2,0,1:T(8,128)(2,1)S(1)}, bf16[8,16,256]{2,0,1:T(8,128)(2,1)S(1)}, u32[]{:S(2)}, u32[]{:S(2)}) collective-permute-start(bf16[8,16,256]{2,0,1:T(8,128)(2,1)S(1)} %get-tuple-element.9), channel_id=1, source_target_pairs={{0,4},{4,8},{8,12},{12,16},{16,20},{20,24},{24,28},{1,5},{5,9},{9,... | collective-permute-start | bytes 196616 | tf_op jit(solution)/shard_map/ppermute | solution.py:18
  120.1 5.9 %collective-permute-start.7 = (bf16[4,16,256]{2,1,0:T(8,128)(2,1)S(1)}, bf16[4,16,256]{2,1,0:T(8,128)(2,1)S(1)}, u32[]{:S(2)}, u32[]{:S(2)}) collective-permute-start(bf16[4,16,256]{2,1,0:T(8,128)(2,1)S(1)} %get-tuple-element.8), channel_id=1, source_target_pairs={{4,0},{8,4},{12,8},{16,12},{20,16},{24,20},{28,24},{5,1},{9,5},{13... | collective-permute-start | bytes 98312 | tf_op jit(solution)/shard_map/ppermute | solution.py:19
  121.4 6.1 %collective-permute-start.6 = (bf16[4,16,256]{2,1,0:T(8,128)(2,1)S(1)}, bf16[4,16,256]{2,1,0:T(8,128)(2,1)S(1)}, u32[]{:S(2)}, u32[]{:S(2)}) collective-permute-start(bf16[4,16,256]{2,1,0:T(8,128)(2,1)S(1)} %get-tuple-element.7), channel_id=1, source_target_pairs={{0,4},{4,8},{8,12},{12,16},{16,20},{20,24},{24,28},{1,5},{5,9},{9,... | collective-permute-start | bytes 98312 | tf_op jit(solution)/shard_map/ppermute | solution.py:18
  137.2 20.8 %copy-start.9 = (u32[32]{0:T(128)S(1)}, u32[32]{0:T(128)}, u32[]{:S(2)}) copy-start(u32[32]{0:T(128)} %constant.82) | copy-start | bytes 388
  137.8 28.3 %copy-start.4 = (bf16[256,128]{1,0:T(8,128)(2,1)S(1)}, bf16[256,128]{1,0:T(8,128)(2,1)}, u32[]{:S(2)}) copy-start(bf16[256,128]{1,0:T(8,128)(2,1)} %param.15) | copy-start | bytes 196612
  150.6 15.7 %copy-start.6 = (s32[256]{0:T(256)S(1)}, s32[256]{0:T(256)}, u32[]{:S(2)}) copy-start(s32[256]{0:T(256)} %param.18) | copy-start | bytes 3076
  150.6 15.9 %copy-start.7 = (s32[256]{0:T(256)S(1)}, s32[256]{0:T(256)}, u32[]{:S(2)}) copy-start(s32[256]{0:T(256)} %param.20) | copy-start | bytes 3076
  150.6 14.7 %all-to-all-start.2 = ((bf16[8,64,128]{2,1,0:T(8,128)(2,1)}), bf16[8,64,128]{2,1,0:T(8,128)(2,1)S(1)}, u32[]{:S(2)}, u32[]{:S(2)}) async-start(bf16[8,64,128]{2,1,0:T(8,128)(2,1)} %convolution_convert_fusion), calls=%async_computation.2 | async-start | bytes 262144 | tf_op jit(solution)/shard_map/all_to_all | solution.py:158
Sparse Core Ops, SparseCore 0:
  65.7 16.9 all-gather.2
  97.2 18.4 all-gather.4
where the time goes:
time: 196 us; the launch traced here: 195 us
  waiting for transfers between devices  57.2 us (29%)
  blocking collectives  46 us (23%)
  starting transfers between devices  42.2 us (22%)
  matrix products  15.8 us (8%)
  between operations  14.4 us (7%)
  other arithmetic  11.8 us (6%)
  local copies, waits for them, and re-layouts  7.41 us (4%)
    all_gather x2, waiting for transfers between devices, dilated_convolution(): lax.all_gather(rimmed, 'chan', axis=1, tiled=True)  35.7 us
    ppermute x4, starting transfers between devices, extended(): before = lax.ppermute(last, axis, up)  18.7 us
    unnamed x1, blocking collectives  18.2 us
    all_gather x2, blocking collectives, dilated_convolution(): lax.all_gather(rimmed, 'chan', axis=1, tiled=True)  16.1 us
    dot_general x36, matrix products, dilated_convolution(): jnp.einsum('rcw,co->row', part_in, own_weights[row_tap, col_tap], preferr...  12.4 us
    psum x1, blocking collectives, local(): grad_demand = lax.psum(partial_grad, 'chan')  11.7 us
    all_to_all x1, starting transfers between devices, local(): lax.all_to_all(slot_grads.astype(jnp.bfloat16), 'tile', split_axis=0, con...  7.38 us
    all_to_all x1, starting transfers between devices, local(): lax.all_to_all(send_ids.reshape(tile_count, slot_count), 'tile', split_ax...  7.31 us
  transfers between devices with their start and end apart: 13, of which 11 were waited for; matrix products, arithmetic and copies ran while one was open for 3% of the time, Pallas kernels for 0%

commit v1 on v0

--- a/solution.py
+++ b/solution.py
@@ -146,7 +146,8 @@
         preactivation_gradient, flipped_kernel(dilation4_weight), channel_start, 4
     )
     partial_grad = jnp.sum(inputs_gradient * lift_own[None, :, None], axis=1)
-    grad_demand = lax.psum(partial_grad, "chan")
+    parts = lax.all_gather(partial_grad, "chan", axis=0, tiled=False)
+    grad_demand = parts.sum(axis=0)
     grad_tiles = (
         grad_demand.reshape(row_count // 8, 8, col_count // 16, 16)
         .transpose(0, 2, 1, 3)

time: 196 us -> 190 us (0.969)
  blocking collectives: 46 us -> 39.8 us
    psum x1 -> x0, blocking collectives: 11.7 us -> none  [local(): grad_demand = lax.psum(partial_grad, 'chan')]
    all_gather x0 -> x1, blocking collectives: none -> 5.24 us  [local(): parts = lax.all_gather(partial_grad, 'chan', axis=0, tiled=False)]
where the time goes in v1:
time: 190 us; the launch traced here: 189 us
  waiting for transfers between devices  57.4 us (30%)
  starting transfers between devices  42.4 us (22%)
  blocking collectives  39.8 us (21%)
  matrix products  15.8 us (8%)
  between operations  14.4 us (8%)
  other arithmetic  11.8 us (6%)
  local copies, waits for them, and re-layouts  7.41 us (4%)
    all_gather x2, waiting for transfers between devices, dilated_convolution(): lax.all_gather(rimmed, 'chan', axis=1, tiled=True)  35.7 us
    ppermute x4, starting transfers between devices, extended(): before = lax.ppermute(last, axis, up)  18.7 us
    unnamed x1, blocking collectives  18.6 us
    all_gather x2, blocking collectives, dilated_convolution(): lax.all_gather(rimmed, 'chan', axis=1, tiled=True)  16.1 us
    dot_general x36, matrix products, dilated_convolution(): jnp.einsum('rcw,co->row', part_in, own_weights[row_tap, col_tap], preferr...  12.4 us
    all_to_all x1, starting transfers between devices, local(): lax.all_to_all(slot_grads.astype(jnp.bfloat16), 'tile', split_axis=0, con...  7.59 us
    all_to_all x1, starting transfers between devices, local(): lax.all_to_all(send_ids.reshape(tile_count, slot_count), 'tile', split_ax...  7.31 us
    ppermute x4, waiting for transfers between devices, extended(): before = lax.ppermute(last, axis, up)  6.25 us
  transfers between devices with their start and end apart: 13, of which 11 were waited for; matrix products, arithmetic and copies ran while one was open for 3% of the time, Pallas kernels for 0%

profile of v1, /device:TPU:0, one launch (start us, length us, event | category | flops | bytes accessed | tf_op | source)
XLA Modules:
  0.0 189.0 jit_solution(1828485017414091264)
XLA Ops:
  9.6 1.6 scatter_custom_fusion
  11.8 7.3 %all-to-all-start = ((s32[8,1,64]{2,1,0:T(1,128)}), s32[8,1,64]{2,1,0:T(1,128)S(1)}, u32[]{:S(2)}, u32[]{:S(2)}) async-start(s32[8,1,64]{2,1,0:T(1,128)} %all_to_all.12), calls=%async_computation | async-start | bytes 8192 | tf_op jit(solution)/shard_map/all_to_all | solution.py:114
  19.9 0.9 fusion.42
  20.8 1.7 scatter_custom_fusion.1
  23.2 2.4 %all-to-all-done = s32[8,1,64]{2,1,0:T(1,128)S(1)} async-done(((s32[8,1,64]{2,1,0:T(1,128)}), s32[8,1,64]{2,1,0:T(1,128)S(1)}, u32[]{:S(2)}, u32[]{:S(2)}) %all-to-all-start) | async-done | bytes 2080 | tf_op jit(solution)/shard_map/all_to_all | solution.py:114
  25.6 3.6 %all-to-all-start.1 = ((bf16[8,64,128]{2,1,0:T(8,128)(2,1)}), bf16[8,64,128]{2,1,0:T(8,128)(2,1)S(1)}, u32[]{:S(2)}, u32[]{:S(2)}) async-start(bf16[8,64,128]{2,1,0:T(8,128)(2,1)} %bitcast.24), calls=%async_computation.1 | async-start | bytes 262144 | tf_op jit(solution)/shard_map/all_to_all | solution.py:107
  30.5 5.9 %all-to-all-done.1 = bf16[8,64,128]{2,1,0:T(8,128)(2,1)S(1)} async-done(((bf16[8,64,128]{2,1,0:T(8,128)(2,1)}), bf16[8,64,128]{2,1,0:T(8,128)(2,1)S(1)}, u32[]{:S(2)}, u32[]{:S(2)}) %all-to-all-start.1) | async-done | bytes 131104 | tf_op jit(solution)/shard_map/all_to_all | solution.py:107
  37.2 1.3 collective-permute-start.1
  38.5 4.5 %collective-permute-start = (bf16[4,16,256]{2,1,0:T(8,128)(2,1)S(1)}, bf16[4,16,256]{2,1,0:T(8,128)(2,1)S(1)}, u32[]{:S(2)}, u32[]{:S(2)}) collective-permute-start(bf16[4,16,256]{2,1,0:T(8,128)(2,1)S(1)} %get-tuple-element.13), channel_id=1, source_target_pairs={{0,4},{4,8},{8,12},{12,16},{16,20},{20,24},{24,28},{1,5},{5,9},{9,... | collective-permute-start | bytes 98312 | tf_op jit(solution)/shard_map/ppermute | solution.py:18
  43.1 1.6 collective-permute-done
  44.7 8.6 %all_gather.18 = bf16[24,64,256]{2,1,0:T(8,128)(2,1)S(1)} all-gather(bf16[24,16,256]{2,1,0:T(8,128)(2,1)S(1)} %pad_maximum_fusion.2), channel_id=1, replica_groups=mesh['tile'=8,'chan'=4] {'chan'}, dimensions={1}, use_global_device_ids=true | all-gather | bytes 983040 | tf_op jit(solution)/shard_map/all_gather | solution.py:35
  56.4 1.3 collective-permute-start.3
  57.7 4.9 %collective-permute-start.2 = (bf16[8,16,256]{2,1,0:T(8,128)(2,1)S(1)}, bf16[8,16,256]{2,1,0:T(8,128)(2,1)S(1)}, u32[]{:S(2)}, u32[]{:S(2)}) collective-permute-start(bf16[8,16,256]{2,1,0:T(8,128)(2,1)S(1)} %get-tuple-element.11), channel_id=1, source_target_pairs={{0,4},{4,8},{8,12},{12,16},{16,20},{20,24},{24,28},{1,5},{5,9},{9,... | collective-permute-start | bytes 196616 | tf_op jit(solution)/shard_map/ppermute | solution.py:18
  63.2 1.6 collective-permute-done.2
  65.6 17.1 %all-gather.4.cloned.1.call-done = bf16[32,64,256]{2,1,0:T(8,128)(2,1)} async-done(((bf16[32,16,256]{2,1,0:T(8,128)(2,1)}), bf16[32,64,256]{2,1,0:T(8,128)(2,1)}) %all-gather.4.cloned.1.call-update) | async-done | bytes 1048592 | tf_op jit(solution)/shard_map/all_gather | solution.py:35
  82.7 1.5 fusion.33
  86.9 1.6 fusion.46
  88.6 1.3 collective-permute-start.5
  89.9 4.7 %collective-permute-start.4 = (bf16[8,16,256]{2,0,1:T(8,128)(2,1)S(1)}, bf16[8,16,256]{2,0,1:T(8,128)(2,1)S(1)}, u32[]{:S(2)}, u32[]{:S(2)}) collective-permute-start(bf16[8,16,256]{2,0,1:T(8,128)(2,1)S(1)} %get-tuple-element.9), channel_id=1, source_target_pairs={{0,4},{4,8},{8,12},{12,16},{16,20},{20,24},{24,28},{1,5},{5,9},{9,... | collective-permute-start | bytes 196616 | tf_op jit(solution)/shard_map/ppermute | solution.py:18
  94.7 1.6 collective-permute-done.4
  97.2 18.6 %all-gather.6.cloned.1.call-done = bf16[32,64,256]{2,0,1:T(8,128)(2,1)} async-done(((bf16[32,16,256]{2,0,1:T(8,128)(2,1)}), bf16[32,64,256]{2,0,1:T(8,128)(2,1)}) %all-gather.6.cloned.1.call-update) | async-done | bytes 1048592 | tf_op jit(solution)/shard_map/all_gather | solution.py:35
  115.7 1.8 copy.104
  120.1 1.3 collective-permute-start.7
  121.4 4.5 %collective-permute-start.6 = (bf16[4,16,256]{2,1,0:T(8,128)(2,1)S(1)}, bf16[4,16,256]{2,1,0:T(8,128)(2,1)S(1)}, u32[]{:S(2)}, u32[]{:S(2)}) collective-permute-start(bf16[4,16,256]{2,1,0:T(8,128)(2,1)S(1)} %get-tuple-element.7), channel_id=1, source_target_pairs={{0,4},{4,8},{8,12},{12,16},{16,20},{20,24},{24,28},{1,5},{5,9},{9,... | collective-permute-start | bytes 98312 | tf_op jit(solution)/shard_map/ppermute | solution.py:18
  126.0 1.5 collective-permute-done.6
  127.6 7.5 %all_gather.21 = bf16[24,64,256]{2,1,0:T(8,128)(2,1)S(1)} all-gather(bf16[24,16,256]{2,1,0:T(8,128)(2,1)S(1)} %pad_maximum_fusion.3), channel_id=1, replica_groups=mesh['tile'=8,'chan'=4] {'chan'}, dimensions={1}, use_global_device_ids=true | all-gather | bytes 983040 | tf_op jit(solution)/shard_map/all_gather | solution.py:35
  137.6 5.2 %all-gather = f32[64,256]{1,0:T(8,128)S(1)} all-gather(f32[16,256]{1,0:T(8,128)S(1)} %fusion.6), channel_id=2, replica_groups=mesh['tile'=8,'chan'=4] {'chan'}, dimensions={0}, use_global_device_ids=true | all-gather | bytes 81920 | tf_op jit(solution)/shard_map/all_gather | solution.py:149
  143.1 1.0 convolution_convert_fusion
  144.1 7.6 %all-to-all-start.2 = ((bf16[8,64,128]{2,1,0:T(8,128)(2,1)}), bf16[8,64,128]{2,1,0:T(8,128)(2,1)S(1)}, u32[]{:S(2)}, u32[]{:S(2)}) async-start(bf16[8,64,128]{2,1,0:T(8,128)(2,1)} %convolution_convert_fusion), calls=%async_computation.2 | async-start | bytes 262144 | tf_op jit(solution)/shard_map/all_to_all | solution.py:159
  153.0 6.2 %all-to-all-done.2 = bf16[8,64,128]{2,1,0:T(8,128)(2,1)S(1)} async-done(((bf16[8,64,128]{2,1,0:T(8,128)(2,1)}), bf16[8,64,128]{2,1,0:T(8,128)(2,1)S(1)}, u32[]{:S(2)}, u32[]{:S(2)}) %all-to-all-start.2) | async-done | bytes 131104 | tf_op jit(solution)/shard_map/all_to_all | solution.py:159
  160.5 2.5 %scatter_custom_fusion.2 = f32[512]{0:T(512)S(1)} fusion(s32[256]{0:T(256)} %param.21, f32[256]{0:T(256)S(1)} %bitcast.284, f32[]{:T(128)} %constant.62.clone.1), kind=kCustom, calls=%fused_computation.200 | custom fusion | flops 256 | bytes 2560 | tf_op jit(solution)/shard_map/scatter-add | solution.py:166
  163.0 18.6 %all-reduce.4 = f32[512]{0:T(512)S(1)} all-reduce(f32[512]{0:T(512)S(1)} %scatter_custom_fusion.2), channel_id=3, replica_groups=mesh['tile'=8,'chan'=4] {'tile'}, use_global_device_ids=true, to_apply=%region_9.10.clone | all-reduce | flops 512 | bytes 4096
  (107 shorter events, 23.3 us)
Async XLA Ops:
  6.5 12.6 %copy-start = (f32[256]{0:T(256)S(1)}, f32[256]{0:T(256)}, u32[]{:S(2)}) copy-start(f32[256]{0:T(256)} %param.19) | copy-start | bytes 3076
  6.5 22.7 %copy-start.8 = (f32[64]{0:T(128)S(1)}, f32[64]{0:T(128)}, u32[]{:S(2)}) copy-start(f32[64]{0:T(128)} %param.12) | copy-start | bytes 772
  6.5 30.5 %copy-start.5 = (bf16[16,16,256]{2,1,0:T(8,128)(2,1)S(1)}, bf16[16,16,256]{2,1,0:T(8,128)(2,1)}, u32[]{:S(2)}) copy-start(bf16[16,16,256]{2,1,0:T(8,128)(2,1)} %param.11) | copy-start | bytes 393220
  11.8 13.8 %all-to-all-start = ((s32[8,1,64]{2,1,0:T(1,128)}), s32[8,1,64]{2,1,0:T(1,128)S(1)}, u32[]{:S(2)}, u32[]{:S(2)}) async-start(s32[8,1,64]{2,1,0:T(1,128)} %all_to_all.12), calls=%async_computation | async-start | bytes 8192 | tf_op jit(solution)/shard_map/all_to_all | solution.py:114
  25.6 10.9 %all-to-all-start.1 = ((bf16[8,64,128]{2,1,0:T(8,128)(2,1)}), bf16[8,64,128]{2,1,0:T(8,128)(2,1)S(1)}, u32[]{:S(2)}, u32[]{:S(2)}) async-start(bf16[8,64,128]{2,1,0:T(8,128)(2,1)} %bitcast.24), calls=%async_computation.1 | async-start | bytes 262144 | tf_op jit(solution)/shard_map/all_to_all | solution.py:107
  29.2 53.6 %all-gather.4.cloned.1.call-start = ((), (), s32[]{:S(2)}) async-start(), calls=%async_computation.3 | async-start | bytes 1310720 | tf_op jit(solution)/shard_map/all_gather | solution.py:35
  36.6 16.7 %copy-start.3 = (bf16[3,3,64,64]{3,2,1,0:T(8,128)(2,1)S(1)}, bf16[3,3,64,64]{3,2,1,0:T(8,128)(2,1)}, u32[]{:S(2)}) copy-start(bf16[3,3,64,64]{3,2,1,0:T(8,128)(2,1)} %param.13) | copy-start | bytes 221188
  37.2 5.9 %collective-permute-start.1 = (bf16[4,16,256]{2,1,0:T(8,128)(2,1)S(1)}, bf16[4,16,256]{2,1,0:T(8,128)(2,1)S(1)}, u32[]{:S(2)}, u32[]{:S(2)}) collective-permute-start(bf16[4,16,256]{2,1,0:T(8,128)(2,1)S(1)} %get-tuple-element.14), channel_id=1, source_target_pairs={{4,0},{8,4},{12,8},{16,12},{20,16},{24,20},{28,24},{5,1},{9,5},{13... | collective-permute-start | bytes 98312 | tf_op jit(solution)/shard_map/ppermute | solution.py:19
  38.5 6.1 %collective-permute-start = (bf16[4,16,256]{2,1,0:T(8,128)(2,1)S(1)}, bf16[4,16,256]{2,1,0:T(8,128)(2,1)S(1)}, u32[]{:S(2)}, u32[]{:S(2)}) collective-permute-start(bf16[4,16,256]{2,1,0:T(8,128)(2,1)S(1)} %get-tuple-element.13), channel_id=1, source_target_pairs={{0,4},{4,8},{8,12},{12,16},{16,20},{20,24},{24,28},{1,5},{5,9},{9,... | collective-permute-start | bytes 98312 | tf_op jit(solution)/shard_map/ppermute | solution.py:18
  56.0 26.7 %copy-start.2 = (bf16[3,3,64,64]{3,2,1,0:T(8,128)(2,1)S(1)}, bf16[3,3,64,64]{3,2,1,0:T(8,128)(2,1)}, u32[]{:S(2)}) copy-start(bf16[3,3,64,64]{3,2,1,0:T(8,128)(2,1)} %param.14) | copy-start | bytes 221188
  56.4 6.8 %collective-permute-start.3 = (bf16[8,16,256]{2,1,0:T(8,128)(2,1)S(1)}, bf16[8,16,256]{2,1,0:T(8,128)(2,1)S(1)}, u32[]{:S(2)}, u32[]{:S(2)}) collective-permute-start(bf16[8,16,256]{2,1,0:T(8,128)(2,1)S(1)} %get-tuple-element.12), channel_id=1, source_target_pairs={{4,0},{8,4},{12,8},{16,12},{20,16},{24,20},{28,24},{5,1},{9,5},{13... | collective-permute-start | bytes 196616 | tf_op jit(solution)/shard_map/ppermute | solution.py:19
  57.7 7.1 %collective-permute-start.2 = (bf16[8,16,256]{2,1,0:T(8,128)(2,1)S(1)}, bf16[8,16,256]{2,1,0:T(8,128)(2,1)S(1)}, u32[]{:S(2)}, u32[]{:S(2)}) collective-permute-start(bf16[8,16,256]{2,1,0:T(8,128)(2,1)S(1)} %get-tuple-element.11), channel_id=1, source_target_pairs={{0,4},{4,8},{8,12},{12,16},{16,20},{20,24},{24,28},{1,5},{5,9},{9,... | collective-permute-start | bytes 196616 | tf_op jit(solution)/shard_map/ppermute | solution.py:18
  65.6 50.2 %all-gather.6.cloned.1.call-start = ((), (), s32[]{:S(2)}) async-start(), calls=%async_computation.4 | async-start | bytes 1310720 | tf_op jit(solution)/shard_map/all_gather | solution.py:35
  82.7 1.5 copy-start.1
  88.6 6.2 %collective-permute-start.5 = (bf16[8,16,256]{2,0,1:T(8,128)(2,1)S(1)}, bf16[8,16,256]{2,0,1:T(8,128)(2,1)S(1)}, u32[]{:S(2)}, u32[]{:S(2)}) collective-permute-start(bf16[8,16,256]{2,0,1:T(8,128)(2,1)S(1)} %get-tuple-element.10), channel_id=1, source_target_pairs={{4,0},{8,4},{12,8},{16,12},{20,16},{24,20},{28,24},{5,1},{9,5},{13... | collective-permute-start | bytes 196616 | tf_op jit(solution)/shard_map/ppermute | solution.py:19
  89.9 6.4 %collective-permute-start.4 = (bf16[8,16,256]{2,0,1:T(8,128)(2,1)S(1)}, bf16[8,16,256]{2,0,1:T(8,128)(2,1)S(1)}, u32[]{:S(2)}, u32[]{:S(2)}) collective-permute-start(bf16[8,16,256]{2,0,1:T(8,128)(2,1)S(1)} %get-tuple-element.9), channel_id=1, source_target_pairs={{0,4},{4,8},{8,12},{12,16},{16,20},{20,24},{24,28},{1,5},{5,9},{9,... | collective-permute-start | bytes 196616 | tf_op jit(solution)/shard_map/ppermute | solution.py:18
  120.1 5.9 %collective-permute-start.7 = (bf16[4,16,256]{2,1,0:T(8,128)(2,1)S(1)}, bf16[4,16,256]{2,1,0:T(8,128)(2,1)S(1)}, u32[]{:S(2)}, u32[]{:S(2)}) collective-permute-start(bf16[4,16,256]{2,1,0:T(8,128)(2,1)S(1)} %get-tuple-element.8), channel_id=1, source_target_pairs={{4,0},{8,4},{12,8},{16,12},{20,16},{24,20},{28,24},{5,1},{9,5},{13... | collective-permute-start | bytes 98312 | tf_op jit(solution)/shard_map/ppermute | solution.py:19
  121.4 6.1 %collective-permute-start.6 = (bf16[4,16,256]{2,1,0:T(8,128)(2,1)S(1)}, bf16[4,16,256]{2,1,0:T(8,128)(2,1)S(1)}, u32[]{:S(2)}, u32[]{:S(2)}) collective-permute-start(bf16[4,16,256]{2,1,0:T(8,128)(2,1)S(1)} %get-tuple-element.7), channel_id=1, source_target_pairs={{0,4},{4,8},{8,12},{12,16},{16,20},{20,24},{24,28},{1,5},{5,9},{9,... | collective-permute-start | bytes 98312 | tf_op jit(solution)/shard_map/ppermute | solution.py:18
  137.2 14.5 %copy-start.9 = (u32[32]{0:T(128)S(1)}, u32[32]{0:T(128)}, u32[]{:S(2)}) copy-start(u32[32]{0:T(128)} %constant.82) | copy-start | bytes 388
  143.1 16.9 %copy-start.4 = (bf16[256,128]{1,0:T(8,128)(2,1)S(1)}, bf16[256,128]{1,0:T(8,128)(2,1)}, u32[]{:S(2)}) copy-start(bf16[256,128]{1,0:T(8,128)(2,1)} %param.15) | copy-start | bytes 196612
  144.1 16.0 %copy-start.6 = (s32[256]{0:T(256)S(1)}, s32[256]{0:T(256)}, u32[]{:S(2)}) copy-start(s32[256]{0:T(256)} %param.18) | copy-start | bytes 3076
  144.1 16.3 %copy-start.7 = (s32[256]{0:T(256)S(1)}, s32[256]{0:T(256)}, u32[]{:S(2)}) copy-start(s32[256]{0:T(256)} %param.20) | copy-start | bytes 3076
  144.1 15.1 %all-to-all-start.2 = ((bf16[8,64,128]{2,1,0:T(8,128)(2,1)}), bf16[8,64,128]{2,1,0:T(8,128)(2,1)S(1)}, u32[]{:S(2)}, u32[]{:S(2)}) async-start(bf16[8,64,128]{2,1,0:T(8,128)(2,1)} %convolution_convert_fusion), calls=%async_computation.2 | async-start | bytes 262144 | tf_op jit(solution)/shard_map/all_to_all | solution.py:159
Sparse Core Ops, SparseCore 0:
  65.7 16.9 all-gather.3
  97.2 18.4 all-gather.5
